TPU v7x, 32 devices: a whole 2x2x4 slice. The times are simulated.
32 devices in a mesh: blk: 8 (over z, core), tenant: 4 (over y, x).
Axes of the slice: x: 2, y: 2, z: 4, core: 2. Of those that a mesh axis runs over, the one named last changes fastest.
Arguments:
- history_u: bfloat16 [4, 1024, 4096], P('tenant', 'blk'), may hold values from -6 to 6
- span_gate: bfloat16 [4, 64, 4096], P('tenant', 'blk'), may hold values from -6 to 6
- span_key: bfloat16 [4, 64, 4096], P('tenant', 'blk'), may hold values from -6 to 6
- span_value: bfloat16 [4, 64, 4096], P('tenant', 'blk'), may hold values from -6 to 6
- filter_taps: bfloat16 [1088, 256], P(('blk', 'tenant'))
- skip_bias: bfloat16 [4096], P(('blk', 'tenant')), may hold values from -6 to 6
- lengths: int32 [4], P('tenant'), may hold values from 1 to 1024, as said below
- page_owner: int32 [4, 8, 1], P('tenant'), may hold values from 0 to 7; in each aligned block of 8 rows (0 to 7, 8 to 15, ..., all dimensions but the last counted through in order) at most 2 rows name the same one
Outputs:
- mixed: bfloat16 [4, 64, 4096], P('tenant', 'blk')
- new_pool: bfloat16 [4, 128, 4096], P('tenant', 'blk')
Inputs may be any that keep to these rules, and one draw needn't show every extreme that they name: `lengths`: lengths are at least 1, and some tenant uses all 1024 cached positions in every draw. `page_owner`: among the 8 pages of one tenant no device is named more than 2 times, and some device is named exactly 2 times.
All inputs are finite; a program needn't handle non-finite values.
Results may differ from a plain program's by a relative error of at most 0.0044.
Values may be sent and summed in bfloat16 or wider, within the bound.
No kernel may reach another device: no remote copies, remote signals or barrier semaphores. Data moves between devices by JAX's collectives and lax.ppermute only.
A program may use at most 128 MiB of HBM per device.

v0:
```python
import jax
import jax.numpy as jnp
from jax import lax
from jax.sharding import PartitionSpec as P

PAGE = 8
PAGES_DEV = 1
MOST = 2


def toeplitz(window, tile_rows, groups):
    reversed_taps = jnp.transpose(window[::-1])
    repeated = jnp.tile(reversed_taps, (1, tile_rows))
    trimmed = repeated[:, tile_rows - 1 : tile_rows - 1 + tile_rows * (2 * tile_rows - 2)]
    return trimmed.reshape(groups, tile_rows, 2 * tile_rows - 2)[:, :, :tile_rows]


def tile_table(padded_filter, starts, tile_rows, groups):

    def one_window(start):
        window = lax.dynamic_slice_in_dim(padded_filter, start, 2 * tile_rows - 1, 0)
        return toeplitz(window, tile_rows, groups)

    return jax.vmap(one_window)(starts)


def blocked_convolution(table, sources_reversed, target_blocks, source_blocks):

    def per_target(target_index):
        tiles = lax.dynamic_slice_in_dim(table, target_index, source_blocks, 0)
        return jnp.einsum(
            "mgab,mbgc->agc", tiles, sources_reversed, preferred_element_type=jnp.float32
        )

    return lax.map(per_target, jnp.arange(target_blocks, dtype=jnp.int32))


def per_device(
    history_u, span_gate, span_key, span_value, filter_taps, skip_bias, lengths, page_owner
):
    cycle_size = lax.axis_size("blk")
    own_index = lax.axis_index("blk")
    history = history_u[0]
    gate_rows = span_gate[0]
    history_rows, width = history.shape
    span_rows = gate_rows.shape[0]
    span_total = span_rows * cycle_size
    groups = filter_taps.shape[1]
    group_size = width // groups
    taps_all, bias_all = (
        lax.all_gather(filter_taps, ("blk", "tenant"), axis=0, tiled=True),
        lax.all_gather(skip_bias, ("blk", "tenant"), axis=0, tiled=True),
    )
    length = lengths[0]
    own_rows = (span_key[0].astype(jnp.float32) * span_value[0].astype(jnp.float32)).astype(
        jnp.bfloat16
    )
    tile_rows = min(32, history_rows, span_total)
    target_blocks = span_total // tile_rows
    column_history, column_span = (
        lax.all_to_all(history, "blk", split_axis=1, concat_axis=0, tiled=True),
        lax.all_to_all(own_rows, "blk", split_axis=1, concat_axis=0, tiled=True),
    )
    column_width = width // cycle_size
    local_groups = column_width // group_size
    full_rows = column_history.shape[0]
    filter_rows_all = full_rows + span_total
    taps_local = lax.dynamic_slice_in_dim(taps_all, own_index * local_groups, local_groups, 1)
    masked_columns = jnp.where(
        jnp.arange(full_rows, dtype=jnp.int32)[:, None] < length,
        column_history,
        jnp.zeros_like(column_history),
    )
    sequence = jnp.concatenate(
        [masked_columns, jnp.zeros((span_total, column_width), jnp.bfloat16)], axis=0
    )
    sequence = lax.dynamic_update_slice(sequence, column_span, (length, jnp.int32(0)))
    source_blocks = filter_rows_all // tile_rows
    padded_filter = jnp.concatenate(
        [jnp.zeros((filter_rows_all, local_groups), jnp.bfloat16), taps_local], axis=0
    )
    offsets = jnp.arange(target_blocks + source_blocks - 1, dtype=jnp.int32) - (source_blocks - 1)
    starts = length + offsets * tile_rows - (tile_rows - 1) + filter_rows_all
    table = tile_table(padded_filter, starts, tile_rows, local_groups)
    sources_reversed = sequence.reshape(source_blocks, tile_rows, local_groups, group_size)[::-1]
    column_out = blocked_convolution(table, sources_reversed, target_blocks, source_blocks).reshape(
        span_total, column_width
    )
    convolved = lax.all_to_all(column_out, "blk", split_axis=0, concat_axis=1, tiled=True)
    mixed = (
        gate_rows.astype(jnp.float32)
        * (convolved + bias_all.astype(jnp.float32)[None, :] * own_rows.astype(jnp.float32))
    ).astype(jnp.bfloat16)
    owners = page_owner[0, :, 0]
    page_count = owners.shape[0]
    onehot = (owners[:, None] == jnp.arange(cycle_size, dtype=jnp.int32)[None, :]).astype(jnp.int32)
    before = jnp.cumsum(onehot, axis=0) - onehot
    slot_rank = jnp.sum(before * onehot, axis=1)
    selector = (
        (owners[None, :] == own_index)
        & (slot_rank[None, :] == jnp.arange(MOST, dtype=jnp.int32)[:, None])
    ).astype(jnp.bfloat16)
    local_pages = own_rows.reshape(PAGES_DEV, PAGE * width)
    targets_of = lax.dynamic_slice_in_dim(owners, own_index * PAGES_DEV, PAGES_DEV, 0)
    send_mask = targets_of[None, :] == jnp.arange(cycle_size, dtype=jnp.int32)[:, None]
    outgoing = jnp.where(
        send_mask[:, :, None], local_pages[None, :, :], jnp.zeros((), jnp.bfloat16)
    )
    incoming = lax.all_to_all(outgoing, "blk", split_axis=0, concat_axis=0, tiled=True)
    arrived = incoming.reshape(page_count, PAGE * width)
    new_pool = jnp.dot(selector, arrived, preferred_element_type=jnp.float32).astype(jnp.bfloat16)
    return (mixed[None], new_pool.reshape(MOST * PAGE, width)[None])


def solution(mesh):
    return jax.shard_map(
        per_device,
        mesh=mesh,
        in_specs=(
            P("tenant", "blk", None),
            P("tenant", "blk", None),
            P("tenant", "blk", None),
            P("tenant", "blk", None),
            P(("blk", "tenant"), None),
            P(("blk", "tenant")),
            P("tenant"),
            P("tenant", None, None),
        ),
        out_specs=(P("tenant", "blk", None), P("tenant", "blk", None)),
        check_vma=False,
    )
```

profile of v0, /device:TPU:0, one launch (start us, length us, event | category | flops | bytes accessed | tf_op | source)
XLA Modules:
  0.0 384.5 jit_solution(1890351494734139457)
XLA Ops:
  0.6 1.3 constant_dynamic-slice_fusion.1
  2.6 1.5 multiply_convert_fusion.1
  5.0 0.9 broadcast_select_fusion
  6.5 3.8 reduce
  10.3 1.2 reshape.183
  11.4 6.3 %all-to-all-start.3 = ((bf16[8,2,16384]{2,1,0:T(2,128)(2,1)}), bf16[8,2,16384]{2,1,0:T(2,128)(2,1)S(1)}, u32[]{:S(2)}, u32[]{:S(2)}) async-start(bf16[8,2,16384]{2,1,0:T(2,128)(2,1)} %reshape.183), calls=%async_computation.3 | async-start | bytes 1048576 | tf_op jit(solution)/shard_map/all_to_all | solution.py:109
  17.8 74.8 %all-gather = bf16[32,34,256]{2,1,0:T(8,128)(2,1)S(1)} all-gather(bf16[1,34,256]{2,1,0:T(8,128)(2,1)} %bitcast.67), channel_id=1, replica_groups=mesh['blk'=8,'tenant'=4] {'blk','tenant'}, dimensions={0}, use_global_device_ids=true | all-gather | bytes 574464 | tf_op jit(solution)/shard_map/all_gather | solution.py:51
  93.4 1.3 copy.31
  95.0 3.7 all-to-all-start
  98.8 65.2 %while.12 = (s32[]{:T(128)}, bf16[2176,32]{1,0:T(8,128)(2,1)S(1)}, s32[35,2]{0,1:T(2,128)S(1)}, bf16[35,63,32]{2,1,0:T(8,128)(2,1)}, s32[]{:T(128)}) while((s32[]{:T(128)}, bf16[2176,32]{1,0:T(8,128)(2,1)S(1)}, s32[35,2]{0,1:T(2,128)S(1)}, bf16[35,63,32]{2,1,0:T(8,128)(2,1)}, s32[]{:T(128)}) %tuple.37), condition=%wide.while_cond, body=%wide.while_body.sunk | while | flops 2 | bytes 21529 | solution.py:21
  99.4 1.3 bitcast_dynamic-update-slice_fusion.2
  101.3 1.2 bitcast_dynamic-update-slice_fusion.2
  103.1 1.2 bitcast_dynamic-update-slice_fusion.2
  105.0 1.2 bitcast_dynamic-update-slice_fusion.2
  106.8 1.3 bitcast_dynamic-update-slice_fusion.2
  108.7 1.2 bitcast_dynamic-update-slice_fusion.2
  110.6 1.2 bitcast_dynamic-update-slice_fusion.2
  112.4 1.3 bitcast_dynamic-update-slice_fusion.2
  114.3 1.2 bitcast_dynamic-update-slice_fusion.2
  116.2 1.2 bitcast_dynamic-update-slice_fusion.2
  118.0 1.2 bitcast_dynamic-update-slice_fusion.2
  119.9 1.3 bitcast_dynamic-update-slice_fusion.2
  121.8 1.2 bitcast_dynamic-update-slice_fusion.2
  123.6 1.2 bitcast_dynamic-update-slice_fusion.2
  125.5 1.2 bitcast_dynamic-update-slice_fusion.2
  127.3 1.3 bitcast_dynamic-update-slice_fusion.2
  129.2 1.2 bitcast_dynamic-update-slice_fusion.2
  131.1 1.2 bitcast_dynamic-update-slice_fusion.2
  132.9 1.2 bitcast_dynamic-update-slice_fusion.2
  134.8 1.3 bitcast_dynamic-update-slice_fusion.2
  136.7 1.2 bitcast_dynamic-update-slice_fusion.2
  138.5 1.3 bitcast_dynamic-update-slice_fusion.2
  140.4 1.2 bitcast_dynamic-update-slice_fusion.2
  142.2 1.2 bitcast_dynamic-update-slice_fusion.2
  144.1 1.2 bitcast_dynamic-update-slice_fusion.2
  146.0 1.2 bitcast_dynamic-update-slice_fusion.2
  147.8 1.3 bitcast_dynamic-update-slice_fusion.2
  149.7 1.3 bitcast_dynamic-update-slice_fusion.2
  151.6 1.2 bitcast_dynamic-update-slice_fusion.2
  153.4 1.2 bitcast_dynamic-update-slice_fusion.2
  155.3 1.2 bitcast_dynamic-update-slice_fusion.2
  157.1 1.2 bitcast_dynamic-update-slice_fusion.2
  159.0 1.2 bitcast_dynamic-update-slice_fusion.2
  160.9 1.2 bitcast_dynamic-update-slice_fusion.2
  162.7 1.2 bitcast_dynamic-update-slice_fusion.2
  164.0 2.3 rev.6
  166.6 4.7 %tile.4 = bf16[35,32,32,63]{3,2,1,0:T(8,128)(2,1)} broadcast(bf16[35,32,63]{2,1,0:T(8,128)(2,1)S(1)} %copy.30), dimensions={0,1,3} | broadcast | bytes 4656960 | tf_op jit(solution)/shard_map/vmap()/tile | solution.py:13
  171.3 16.1 %tile.10 = bf16[35,32,2016]{2,1,0:T(8,128)(2,1)} reshape(bf16[35,32,32,63]{3,2,1,0:T(8,128)(2,1)} %tile.4) | data formatting | bytes 9031680 | tf_op jit(solution)/shard_map/vmap()/tile | solution.py:13
  187.4 6.9 %slice.19 = bf16[35,32,1984]{2,1,0:T(8,128)(2,1)} slice(bf16[35,32,2016]{2,1,0:T(8,128)(2,1)} %tile.10), slice={[0:35], [0:32], [31:2015]} | slice | bytes 8888320 | tf_op jit(solution)/shard_map/vmap()/slice | solution.py:14
  194.4 31.4 %reshape.155 = bf16[35,32,32,62]{3,2,1,0:T(8,128)(2,1)} reshape(bf16[35,32,1984]{2,1,0:T(8,128)(2,1)} %slice.19) | data formatting | bytes 8888320 | tf_op jit(solution)/shard_map/vmap()/reshape | solution.py:15
  225.8 14.3 %copy.34 = bf16[35,32,32,32]{0,2,3,1:T(8,128)(2,1)} copy(bf16[35,32,32,32]{3,2,1,0:T(8,128)(2,1)} %bitcast.60) | data formatting | bytes 4587520 | tf_op jit(solution)/shard_map/while | solution.py:35
  240.1 66.1 %all-gather.1 = bf16[32,1,128]{2,1,0:T(2,128)(2,1)S(1)} all-gather(bf16[1,1,128]{2,1,0:T(2,128)(2,1)S(1)} %bitcast.70), channel_id=1, replica_groups=mesh['blk'=8,'tenant'=4] {'blk','tenant'}, dimensions={0}, use_global_device_ids=true | all-gather | bytes 8448 | tf_op jit(solution)/shard_map/all_gather | solution.py:52
  307.1 3.6 all-to-all-start.1
  311.5 4.8 %all-to-all-done.1 = bf16[8,8,512]{2,0,1:T(8,128)(2,1)S(1)} async-done(((bf16[8,8,512]{2,0,1:T(8,128)(2,1)}), bf16[8,8,512]{2,0,1:T(8,128)(2,1)S(1)}, u32[]{:S(2)}, u32[]{:S(2)}) %all-to-all-start.1) | async-done | bytes 65568 | tf_op jit(solution)/shard_map/all_to_all | solution.py:62
  317.4 4.8 %reshape.156 = bf16[34,32,32,16]{1,0,3,2:T(8,128)(2,1)} reshape(bf16[1088,512]{0,1:T(8,128)(2,1)S(1)} %copy.33) | data formatting | bytes 2228224 | tf_op jit(solution)/shard_map/reshape | solution.py:85
  322.2 20.3 %rev.7 = bf16[34,32,32,16]{1,0,3,2:T(8,128)(2,1)} reverse(bf16[34,32,32,16]{1,0,3,2:T(8,128)(2,1)} %reshape.156), dimensions={0} | reverse | bytes 2228224 | tf_op jit(solution)/shard_map/rev | solution.py:85
  342.5 8.7 %copy.35 = bf16[34,32,32,16]{0,3,1,2:T(8,128)(2,1)} copy(bf16[34,32,32,16]{1,0,3,2:T(8,128)(2,1)} %rev.7) | data formatting | bytes 2228224 | tf_op jit(solution)/shard_map/while | solution.py:35
  351.2 19.5 %while.11 = (s32[]{:T(128)}, f32[2,32,32,16]{1,3,2,0:T(8,128)S(1)}, s32[2]{0:T(128)S(1)}, bf16[35,32,32,32]{0,2,3,1:T(8,128)(2,1)}, bf16[34,32,32,16]{0,3,1,2:T(8,128)(2,1)}, /*index=5*/s32[]{:T(128)}, s32[]{:T(128)}, s32[]{:T(128)}) while((s32[]{:T(128)}, f32[2,32,32,16]{1,3,2,0:T(8,128)S(1)}, s32[2]{0:T(128)S(1)}, ...), condition=%wide.region_1.2_spmd, body=%wide.region_0.1_spmd.sunk | while | flops 35651588 | bytes 3670155 | solution.py:35
  354.0 7.0 %fusion.23 = f32[2,32,32,16]{1,3,2,0:T(8,128)S(1)} fusion(f32[2,32,32,16]{1,3,2,0:T(8,128)S(1)} %get-tuple-element.156, s32[]{:T(128)} %get-tuple-element.155, bf16[34,32,32,16]{0,3,1,2:T(8,128)(2,1)} %get-tuple-element.167, bf16[35,32,32,32]{0,2,3,1:T(8,128)(2,1)} %get-tuple-element.166, s32[]{:T(128)S(6)} %select_n.48), kind=kOutput, calls=%fused_computation.3.clone.1 | convolution fusion | flops 35651584 | bytes 3670024 | tf_op jit(solution)/shard_map/while/body/eval_jaxpr/mgab,mbgc->agc/dot_general | solution.py:31
  363.7 7.0 %fusion.23 = f32[2,32,32,16]{1,3,2,0:T(8,128)S(1)} fusion(f32[2,32,32,16]{1,3,2,0:T(8,128)S(1)} %get-tuple-element.156, s32[]{:T(128)} %get-tuple-element.155, bf16[34,32,32,16]{0,3,1,2:T(8,128)(2,1)} %get-tuple-element.167, bf16[35,32,32,32]{0,2,3,1:T(8,128)(2,1)} %get-tuple-element.166, s32[]{:T(128)S(6)} %select_n.48), kind=kOutput, calls=%fused_computation.3.clone.1 | convolution fusion | flops 35651584 | bytes 3670024 | tf_op jit(solution)/shard_map/while/body/eval_jaxpr/mgab,mbgc->agc/dot_general | solution.py:31
  371.6 1.3 all_to_all.50
  372.9 3.4 all-to-all-start.2
  377.7 5.3 %all-to-all-done.2 = f32[8,8,512]{2,1,0:T(8,128)S(1)} async-done(((f32[8,8,512]{2,1,0:T(8,128)}), f32[8,8,512]{2,1,0:T(8,128)S(1)}, u32[]{:S(2)}, u32[]{:S(2)}) %all-to-all-start.2) | async-done | bytes 131104 | tf_op jit(solution)/shard_map/all_to_all | solution.py:89
  383.0 1.5 multiply_convert_fusion
  (111 shorter events, 30.6 us)
Async XLA Ops:
  0.6 92.8 %copy-start = (bf16[1,128,4096]{2,1,0:T(8,128)(2,1)S(1)}, bf16[1,128,4096]{2,1,0:T(8,128)(2,1)}, u32[]{:S(2)}) copy-start(bf16[1,128,4096]{2,1,0:T(8,128)(2,1)} %param.10) | copy-start | bytes 3145732
  11.4 83.6 %all-to-all-start.3 = ((bf16[8,2,16384]{2,1,0:T(2,128)(2,1)}), bf16[8,2,16384]{2,1,0:T(2,128)(2,1)S(1)}, u32[]{:S(2)}, u32[]{:S(2)}) async-start(bf16[8,2,16384]{2,1,0:T(2,128)(2,1)} %reshape.183), calls=%async_computation.3 | async-start | bytes 1048576 | tf_op jit(solution)/shard_map/all_to_all | solution.py:109
  95.0 212.0 %all-to-all-start = ((bf16[128,8,512]{0,2,1:T(8,128)(2,1)}), bf16[128,8,512]{0,2,1:T(8,128)(2,1)S(1)}, u32[]{:S(2)}, u32[]{:S(2)}) async-start(bf16[128,8,512]{0,2,1:T(8,128)(2,1)} %bitcast.8), calls=%async_computation | async-start | bytes 2097152 | tf_op jit(solution)/shard_map/all_to_all | solution.py:61
  225.8 14.3 %copy-start.4 = (bf16[128]{0:T(256)(128)(2,1)S(1)}, bf16[128]{0:T(256)(128)(2,1)}, u32[]{:S(2)}) copy-start(bf16[128]{0:T(256)(128)(2,1)} %param.15) | copy-start | bytes 772
  225.8 80.4 %copy-start.3 = (s32[1,8,1]{1,2,0:T(1,128)S(1)}, s32[1,8,1]{1,2,0:T(1,128)}, u32[]{:S(2)}) copy-start(s32[1,8,1]{1,2,0:T(1,128)} %param.17) | copy-start | bytes 100
  307.1 9.2 %all-to-all-start.1 = ((bf16[8,8,512]{2,0,1:T(8,128)(2,1)}), bf16[8,8,512]{2,0,1:T(8,128)(2,1)S(1)}, u32[]{:S(2)}, u32[]{:S(2)}) async-start(bf16[8,8,512]{2,0,1:T(8,128)(2,1)} %bitcast.11), calls=%async_computation.1 | async-start | bytes 131072 | tf_op jit(solution)/shard_map/all_to_all | solution.py:62
  342.5 8.7 %copy-start.1 = (f32[2,32,32,16]{1,3,2,0:T(8,128)S(1)}, f32[2,32,32,16]{1,3,2,0:T(8,128)}, u32[]{:S(2)}) copy-start(f32[2,32,32,16]{1,3,2,0:T(8,128)} %custom-call) | copy-start | bytes 393220
  351.2 31.8 %copy-start.2 = (bf16[1,8,4096]{2,1,0:T(8,128)(2,1)S(1)}, bf16[1,8,4096]{2,1,0:T(8,128)(2,1)}, u32[]{:S(2)}) copy-start(bf16[1,8,4096]{2,1,0:T(8,128)(2,1)} %param.11) | copy-start | bytes 196612
  372.9 10.1 %all-to-all-start.2 = ((f32[8,8,512]{2,1,0:T(8,128)}), f32[8,8,512]{2,1,0:T(8,128)S(1)}, u32[]{:S(2)}, u32[]{:S(2)}) async-start(f32[8,8,512]{2,1,0:T(8,128)} %all_to_all.50), calls=%async_computation.2 | async-start | bytes 262144 | tf_op jit(solution)/shard_map/all_to_all | solution.py:89
where the time goes:
time: 387 us; the launch traced here: 385 us
  local copies, waits for them, and re-layouts  187 us (48%)
  blocking collectives  141 us (36%)
  starting transfers between devices  17 us (4%)
  matrix products  14.7 us (4%)
  waiting for transfers between devices  10.1 us (3%)
  other arithmetic  8.95 us (2%)
  loops' own time  4.23 us (1%)
    all_gather x1, blocking collectives, per_device(): lax.all_gather(filter_taps, ('blk', 'tenant'), axis=0, tiled=True)  74.8 us
    all_gather x1, blocking collectives, per_device(): lax.all_gather(skip_bias, ('blk', 'tenant'), axis=0, tiled=True)  66.1 us
    gather x105, local copies, waits for them, and re-layouts  65.1 us
    reshape x1, local copies, waits for them, and re-layouts, toeplitz(): trimmed.reshape(groups, tile_rows, 2 * tile_rows - 2)[:, :, :tile_rows]  31.4 us
    while x3, local copies, waits for them, and re-layouts, blocked_convolution(): return lax.map(per_target, jnp.arange(target_blocks, dtype=jnp.int32))  23.9 us
    another operation x2, local copies, waits for them, and re-layouts, toeplitz(): repeated = jnp.tile(reversed_taps, (1, tile_rows))  20.8 us
    rev x1, local copies, waits for them, and re-layouts, per_device(): sequence.reshape(source_blocks, tile_rows, local_groups, group_size)[::-1]  20.3 us
    dot_general x2, matrix products, per_target(): jnp.einsum('mgab,mbgc->agc', tiles, sources_reversed, preferred_element_t...  14 us
  transfers between devices with their start and end apart: 4, of which 2 were waited for; matrix products, arithmetic and copies ran while one was open for 38% of the time, Pallas kernels for 0%

commit v1 on v0

--- a/solution.py
+++ b/solution.py
@@ -6,6 +6,28 @@
 PAGE = 8
 PAGES_DEV = 1
 MOST = 2
+
+
+def save_heads_for(array_here, row_dim):
+    opened = list(array_here.shape[1:])
+    opened[row_dim] *= array_here.shape[0]
+    return jnp.moveaxis(array_here, 0, row_dim).reshape(opened)
+
+
+def _see_skins(u_in, lane_axis):
+    cores_n = lax.axis_size(lane_axis)
+    arr_now = u_in[None]
+    for dd in range(cores_n.bit_length() - 1):
+        v_next = 1 << dd
+        formed = lax.ppermute(arr_now, lane_axis, [(jj, jj ^ v_next) for jj in range(cores_n)])
+        res = jnp.stack([arr_now, formed], 0)
+        found_now = lax.axis_index(lane_axis) >> dd & 1
+        arr_now = jnp.where(found_now == 0, res, res[::-1]).reshape(-1, *u_in.shape)
+    return arr_now
+
+
+def switch_waves(unit, xx, where_dim):
+    return save_heads_for(_see_skins(unit, xx), where_dim)
 
 
 def toeplitz(window, tile_rows, groups):
@@ -49,7 +71,7 @@
     group_size = width // groups
     taps_all, bias_all = (
         lax.all_gather(filter_taps, ("blk", "tenant"), axis=0, tiled=True),
-        lax.all_gather(skip_bias, ("blk", "tenant"), axis=0, tiled=True),
+        switch_waves(skip_bias, ("blk", "tenant"), 0),
     )
     length = lengths[0]
     own_rows = (span_key[0].astype(jnp.float32) * span_value[0].astype(jnp.float32)).astype(

time: 387 us -> 344 us (0.89)
  blocking collectives: 141 us -> 74.8 us
  waiting for transfers between devices: 10.1 us -> 25.6 us
  starting transfers between devices: 17 us -> 25.2 us
    all_gather x1 -> x0, blocking collectives: 66.1 us -> none  [per_device(): lax.all_gather(skip_bias, ('blk', 'tenant'), axis=0, tiled=True)]
    ppermute x0 -> x5, waiting for transfers between devices: none -> 15.5 us  [_see_skins(): lax.ppermute(arr_now, lane_axis, [(jj, jj ^ v_next) for jj in range(cores...]
    ppermute x0 -> x5, starting transfers between devices: none -> 9.64 us  [_see_skins(): lax.ppermute(arr_now, lane_axis, [(jj, jj ^ v_next) for jj in range(cores...]
  transfers between devices with their start and end apart: 4 -> 9, of which waited for: 2 -> 4; matrix products, arithmetic and copies ran while one was open for 38% -> 46% of each run, Pallas kernels for 0% -> 0%
where the time goes in v1:
time: 344 us; the launch traced here: 342 us
  local copies, waits for them, and re-layouts  187 us (54%)
  blocking collectives  74.8 us (22%)
  waiting for transfers between devices  25.6 us (7%)
  starting transfers between devices  25.2 us (7%)
  matrix products  14.7 us (4%)
  other arithmetic  9.01 us (3%)
  loops' own time  3.9 us (1%)
    all_gather x1, blocking collectives, per_device(): lax.all_gather(filter_taps, ('blk', 'tenant'), axis=0, tiled=True)  74.8 us
    gather x105, local copies, waits for them, and re-layouts  65.1 us
    reshape x1, local copies, waits for them, and re-layouts, toeplitz(): trimmed.reshape(groups, tile_rows, 2 * tile_rows - 2)[:, :, :tile_rows]  31.4 us
    while x3, local copies, waits for them, and re-layouts, blocked_convolution(): return lax.map(per_target, jnp.arange(target_blocks, dtype=jnp.int32))  23.9 us
    another operation x2, local copies, waits for them, and re-layouts, toeplitz(): repeated = jnp.tile(reversed_taps, (1, tile_rows))  20.9 us
    rev x1, local copies, waits for them, and re-layouts, per_device(): sequence.reshape(source_blocks, tile_rows, local_groups, group_size)[::-1]  20.2 us
    ppermute x5, waiting for transfers between devices, _see_skins(): lax.ppermute(arr_now, lane_axis, [(jj, jj ^ v_next) for jj in range(cores...  15.5 us
    dot_general x2, matrix products, per_target(): jnp.einsum('mgab,mbgc->agc', tiles, sources_reversed, preferred_element_t...  14 us
  transfers between devices with their start and end apart: 9, of which 4 were waited for; matrix products, arithmetic and copies ran while one was open for 46% of the time, Pallas kernels for 0%

profile of v1, /device:TPU:0, one launch (start us, length us, event | category | flops | bytes accessed | tf_op | source)
XLA Modules:
  0.0 341.6 jit_solution(15793917632358611750)
XLA Ops:
  0.6 3.0 collective-permute-start
  5.5 1.5 multiply_convert_fusion.1
  9.4 3.8 %reduce = bf16[8,32768]{1,0:T(8,128)(2,1)S(1)} reduce(bf16[8,1,32768]{2,1,0:T(2,128)(2,1)S(1)} %broadcast_select_fusion, bf16[]{:T(256)} %broadcast.143), dimensions={1}, to_apply=%broadcast_select_fusion.reduce_sub_computation | reduce | bytes 1048578 | tf_op jit(solution)/shard_map/jit(_where)/select_n | solution.py:128
  14.4 4.9 %all-to-all-start.3 = ((bf16[8,2,16384]{2,1,0:T(2,128)(2,1)}), bf16[8,2,16384]{2,1,0:T(2,128)(2,1)S(1)}, u32[]{:S(2)}, u32[]{:S(2)}) async-start(bf16[8,2,16384]{2,1,0:T(2,128)(2,1)} %reshape.203), calls=%async_computation.3 | async-start | bytes 1048576 | tf_op jit(solution)/shard_map/all_to_all | solution.py:131
  19.3 74.8 %all-gather = bf16[32,34,256]{2,1,0:T(8,128)(2,1)S(1)} all-gather(bf16[1,34,256]{2,1,0:T(8,128)(2,1)} %bitcast.87), channel_id=1, replica_groups=mesh['blk'=8,'tenant'=4] {'blk','tenant'}, dimensions={0}, use_global_device_ids=true | all-gather | bytes 574464 | tf_op jit(solution)/shard_map/all_gather | solution.py:73
  95.2 65.2 %while.12 = (s32[]{:T(128)}, bf16[2176,32]{1,0:T(8,128)(2,1)S(1)}, s32[35,2]{0,1:T(2,128)S(1)}, bf16[35,63,32]{2,1,0:T(8,128)(2,1)}, s32[]{:T(128)}) while((s32[]{:T(128)}, bf16[2176,32]{1,0:T(8,128)(2,1)S(1)}, s32[35,2]{0,1:T(2,128)S(1)}, bf16[35,63,32]{2,1,0:T(8,128)(2,1)}, s32[]{:T(128)}) %tuple.40), condition=%wide.while_cond, body=%wide.while_body.sunk | while | flops 2 | bytes 21529 | solution.py:43
  95.8 1.2 bitcast_dynamic-update-slice_fusion.2
  97.7 1.2 bitcast_dynamic-update-slice_fusion.2
  99.6 1.2 bitcast_dynamic-update-slice_fusion.2
  101.4 1.2 bitcast_dynamic-update-slice_fusion.2
  103.3 1.2 bitcast_dynamic-update-slice_fusion.2
  105.1 1.2 bitcast_dynamic-update-slice_fusion.2
  107.0 1.2 bitcast_dynamic-update-slice_fusion.2
  108.9 1.2 bitcast_dynamic-update-slice_fusion.2
  110.7 1.2 bitcast_dynamic-update-slice_fusion.2
  112.6 1.2 bitcast_dynamic-update-slice_fusion.2
  114.5 1.2 bitcast_dynamic-update-slice_fusion.2
  116.3 1.2 bitcast_dynamic-update-slice_fusion.2
  118.2 1.2 bitcast_dynamic-update-slice_fusion.2
  120.1 1.2 bitcast_dynamic-update-slice_fusion.2
  121.9 1.2 bitcast_dynamic-update-slice_fusion.2
  123.8 1.2 bitcast_dynamic-update-slice_fusion.2
  125.6 1.2 bitcast_dynamic-update-slice_fusion.2
  127.5 1.2 bitcast_dynamic-update-slice_fusion.2
  129.4 1.2 bitcast_dynamic-update-slice_fusion.2
  131.2 1.2 bitcast_dynamic-update-slice_fusion.2
  133.1 1.2 bitcast_dynamic-update-slice_fusion.2
  134.9 1.2 bitcast_dynamic-update-slice_fusion.2
  136.8 1.2 bitcast_dynamic-update-slice_fusion.2
  138.7 1.2 bitcast_dynamic-update-slice_fusion.2
  140.5 1.2 bitcast_dynamic-update-slice_fusion.2
  142.4 1.2 bitcast_dynamic-update-slice_fusion.2
  144.3 1.2 bitcast_dynamic-update-slice_fusion.2
  146.1 1.2 bitcast_dynamic-update-slice_fusion.2
  148.0 1.2 bitcast_dynamic-update-slice_fusion.2
  149.8 1.2 bitcast_dynamic-update-slice_fusion.2
  151.7 1.2 bitcast_dynamic-update-slice_fusion.2
  153.6 1.2 bitcast_dynamic-update-slice_fusion.2
  155.4 1.2 bitcast_dynamic-update-slice_fusion.2
  157.3 1.2 bitcast_dynamic-update-slice_fusion.2
  159.2 1.2 bitcast_dynamic-update-slice_fusion.2
  160.4 1.3 copy.31
  161.9 3.7 %all-to-all-start = ((bf16[128,8,512]{0,2,1:T(8,128)(2,1)}), bf16[128,8,512]{0,2,1:T(8,128)(2,1)S(1)}, u32[]{:S(2)}, u32[]{:S(2)}) async-start(bf16[128,8,512]{0,2,1:T(8,128)(2,1)} %bitcast.8), calls=%async_computation | async-start | bytes 2097152 | tf_op jit(solution)/shard_map/all_to_all | solution.py:83
  166.9 1.8 collective-permute-start.3
  168.9 14.6 %collective-permute-done.3 = bf16[8,128]{1,0:T(8,128)(2,1)S(1)} collective-permute-done((bf16[8,128]{1,0:T(8,128)(2,1)S(1)}, bf16[8,128]{1,0:T(8,128)(2,1)S(1)}, u32[]{:S(2)}, u32[]{:S(2)}) %collective-permute-start.3) | collective-permute-done | bytes 2080 | tf_op jit(solution)/shard_map/ppermute | solution.py:22
  183.5 4.5 %collective-permute-start.4 = (bf16[16,128]{1,0:T(8,128)(2,1)S(1)}, bf16[16,128]{1,0:T(8,128)(2,1)S(1)}, u32[]{:S(2)}, u32[]{:S(2)}) collective-permute-start(bf16[16,128]{1,0:T(8,128)(2,1)S(1)} %get-tuple-element.77), channel_id=1, source_target_pairs={{0,16},{1,17},{2,18},{3,19},{4,20},{5,21},{6,22},{7,23},{8,24},{9,... | collective-permute-start | bytes 12296 | tf_op jit(solution)/shard_map/ppermute | solution.py:22
  188.0 2.3 rev.21
  190.6 4.7 %tile.4 = bf16[35,32,32,63]{3,2,1,0:T(8,128)(2,1)} broadcast(bf16[35,32,63]{2,1,0:T(8,128)(2,1)S(1)} %copy.30), dimensions={0,1,3} | broadcast | bytes 4656960 | tf_op jit(solution)/shard_map/vmap()/tile | solution.py:35
  195.4 16.1 %tile.10 = bf16[35,32,2016]{2,1,0:T(8,128)(2,1)} reshape(bf16[35,32,32,63]{3,2,1,0:T(8,128)(2,1)} %tile.4) | data formatting | bytes 9031680 | tf_op jit(solution)/shard_map/vmap()/tile | solution.py:35
  211.5 7.0 %slice.19 = bf16[35,32,1984]{2,1,0:T(8,128)(2,1)} slice(bf16[35,32,2016]{2,1,0:T(8,128)(2,1)} %tile.10), slice={[0:35], [0:32], [31:2015]} | slice | bytes 8888320 | tf_op jit(solution)/shard_map/vmap()/slice | solution.py:36
  218.4 31.4 %reshape.173 = bf16[35,32,32,62]{3,2,1,0:T(8,128)(2,1)} reshape(bf16[35,32,1984]{2,1,0:T(8,128)(2,1)} %slice.19) | data formatting | bytes 8888320 | tf_op jit(solution)/shard_map/vmap()/reshape | solution.py:37
  249.8 14.3 %copy.34 = bf16[35,32,32,32]{0,2,3,1:T(8,128)(2,1)} copy(bf16[35,32,32,32]{3,2,1,0:T(8,128)(2,1)} %bitcast.80) | data formatting | bytes 4587520 | tf_op jit(solution)/shard_map/while | solution.py:57
  264.7 3.6 %all-to-all-start.1 = ((bf16[8,8,512]{2,0,1:T(8,128)(2,1)}), bf16[8,8,512]{2,0,1:T(8,128)(2,1)S(1)}, u32[]{:S(2)}, u32[]{:S(2)}) async-start(bf16[8,8,512]{2,0,1:T(8,128)(2,1)} %bitcast.11), calls=%async_computation.1 | async-start | bytes 131072 | tf_op jit(solution)/shard_map/all_to_all | solution.py:84
  269.1 4.8 %all-to-all-done.1 = bf16[8,8,512]{2,0,1:T(8,128)(2,1)S(1)} async-done(((bf16[8,8,512]{2,0,1:T(8,128)(2,1)}), bf16[8,8,512]{2,0,1:T(8,128)(2,1)S(1)}, u32[]{:S(2)}, u32[]{:S(2)}) %all-to-all-start.1) | async-done | bytes 65568 | tf_op jit(solution)/shard_map/all_to_all | solution.py:84
  275.0 4.7 %reshape.174 = bf16[34,32,32,16]{1,0,3,2:T(8,128)(2,1)} reshape(bf16[1088,512]{0,1:T(8,128)(2,1)S(1)} %copy.33) | data formatting | bytes 2228224 | tf_op jit(solution)/shard_map/reshape | solution.py:107
  279.8 20.2 %rev.22 = bf16[34,32,32,16]{1,0,3,2:T(8,128)(2,1)} reverse(bf16[34,32,32,16]{1,0,3,2:T(8,128)(2,1)} %reshape.174), dimensions={0} | reverse | bytes 2228224 | tf_op jit(solution)/shard_map/rev | solution.py:107
  300.0 8.7 %copy.35 = bf16[34,32,32,16]{0,3,1,2:T(8,128)(2,1)} copy(bf16[34,32,32,16]{1,0,3,2:T(8,128)(2,1)} %rev.22) | data formatting | bytes 2228224 | tf_op jit(solution)/shard_map/while | solution.py:57
  308.8 19.1 %while.11 = (s32[]{:T(128)}, f32[2,32,32,16]{1,3,2,0:T(8,128)S(1)}, s32[2]{0:T(128)S(1)}, bf16[35,32,32,32]{0,2,3,1:T(8,128)(2,1)}, bf16[34,32,32,16]{0,3,1,2:T(8,128)(2,1)}, /*index=5*/s32[]{:T(128)}, s32[]{:T(128)}, s32[]{:T(128)}) while((s32[]{:T(128)}, f32[2,32,32,16]{1,3,2,0:T(8,128)S(1)}, s32[2]{0:T(128)S(1)}, ...), condition=%wide.region_1.2_spmd, body=%wide.region_0.1_spmd.sunk | while | flops 35651588 | bytes 3670155 | solution.py:57
  311.3 7.0 %fusion.25 = f32[2,32,32,16]{1,3,2,0:T(8,128)S(1)} fusion(f32[2,32,32,16]{1,3,2,0:T(8,128)S(1)} %get-tuple-element.160, s32[]{:T(128)} %get-tuple-element.159, bf16[34,32,32,16]{0,3,1,2:T(8,128)(2,1)} %get-tuple-element.171, bf16[35,32,32,32]{0,2,3,1:T(8,128)(2,1)} %get-tuple-element.170, s32[]{:T(128)S(6)} %select_n.116), kind=kOutput, calls=%fused_computation.3.clone.1 | convolution fusion | flops 35651584 | bytes 3670024 | tf_op jit(solution)/shard_map/while/body/eval_jaxpr/mgab,mbgc->agc/dot_general | solution.py:53
  320.8 7.0 %fusion.25 = f32[2,32,32,16]{1,3,2,0:T(8,128)S(1)} fusion(f32[2,32,32,16]{1,3,2,0:T(8,128)S(1)} %get-tuple-element.160, s32[]{:T(128)} %get-tuple-element.159, bf16[34,32,32,16]{0,3,1,2:T(8,128)(2,1)} %get-tuple-element.171, bf16[35,32,32,32]{0,2,3,1:T(8,128)(2,1)} %get-tuple-element.170, s32[]{:T(128)S(6)} %select_n.116), kind=kOutput, calls=%fused_computation.3.clone.1 | convolution fusion | flops 35651584 | bytes 3670024 | tf_op jit(solution)/shard_map/while/body/eval_jaxpr/mgab,mbgc->agc/dot_general | solution.py:53
  328.7 1.3 all_to_all.50
  330.0 3.4 all-to-all-start.2
  334.8 5.3 %all-to-all-done.2 = f32[8,8,512]{2,1,0:T(8,128)S(1)} async-done(((f32[8,8,512]{2,1,0:T(8,128)}), f32[8,8,512]{2,1,0:T(8,128)S(1)}, u32[]{:S(2)}, u32[]{:S(2)}) %all-to-all-start.2) | async-done | bytes 131104 | tf_op jit(solution)/shard_map/all_to_all | solution.py:111
  340.1 1.5 multiply_convert_fusion
  (131 shorter events, 35.4 us)
Async XLA Ops:
  0.6 159.8 %copy-start = (bf16[1,128,4096]{2,1,0:T(8,128)(2,1)S(1)}, bf16[1,128,4096]{2,1,0:T(8,128)(2,1)}, u32[]{:S(2)}) copy-start(bf16[1,128,4096]{2,1,0:T(8,128)(2,1)} %param.10) | copy-start | bytes 3145732
  0.6 161.1 %collective-permute-start = (bf16[1,128]{1,0:T(2,128)(2,1)}, bf16[1,128]{1,0:T(2,128)(2,1)S(1)}, u32[]{:S(2)}, u32[]{:S(2)}) collective-permute-start(bf16[1,128]{1,0:T(2,128)(2,1)} %bitcast.97), channel_id=1, source_target_pairs={{0,1},{1,0},{2,3},{3,2},{4,5},{5,4},{6,7},{7,6},{8,9},{9,8},{10,11... | collective-permute-start | bytes 776 | tf_op jit(solution)/shard_map/ppermute | solution.py:22
  7.9 153.8 %copy-start.4 = (bf16[128]{0:T(256)(128)(2,1)S(1)}, bf16[128]{0:T(256)(128)(2,1)}, u32[]{:S(2)}) copy-start(bf16[128]{0:T(256)(128)(2,1)} %param.15) | copy-start | bytes 772
  13.2 152.4 %copy-start.3 = (s32[1,8,1]{1,2,0:T(1,128)S(1)}, s32[1,8,1]{1,2,0:T(1,128)}, u32[]{:S(2)}) copy-start(s32[1,8,1]{1,2,0:T(1,128)} %param.17) | copy-start | bytes 100
  14.4 147.4 %all-to-all-start.3 = ((bf16[8,2,16384]{2,1,0:T(2,128)(2,1)}), bf16[8,2,16384]{2,1,0:T(2,128)(2,1)S(1)}, u32[]{:S(2)}, u32[]{:S(2)}) async-start(bf16[8,2,16384]{2,1,0:T(2,128)(2,1)} %reshape.203), calls=%async_computation.3 | async-start | bytes 1048576 | tf_op jit(solution)/shard_map/all_to_all | solution.py:131
  161.8 3.9 %collective-permute-start.1 = (bf16[2,128]{1,0:T(2,128)(2,1)S(1)}, bf16[2,128]{1,0:T(2,128)(2,1)S(1)}, u32[]{:S(2)}, u32[]{:S(2)}) collective-permute-start(bf16[2,128]{1,0:T(2,128)(2,1)S(1)} %bitcast.100), channel_id=1, source_target_pairs={{0,2},{1,3},{2,0},{3,1},{4,6},{5,7},{6,4},{7,5},{8,10},{9,11},{10,... | collective-permute-start | bytes 1544 | tf_op jit(solution)/shard_map/ppermute | solution.py:22
  161.9 102.8 %all-to-all-start = ((bf16[128,8,512]{0,2,1:T(8,128)(2,1)}), bf16[128,8,512]{0,2,1:T(8,128)(2,1)S(1)}, u32[]{:S(2)}, u32[]{:S(2)}) async-start(bf16[128,8,512]{0,2,1:T(8,128)(2,1)} %bitcast.8), calls=%async_computation | async-start | bytes 2097152 | tf_op jit(solution)/shard_map/all_to_all | solution.py:83
  165.7 1.2 collective-permute-start.2
  166.9 16.6 %collective-permute-start.3 = (bf16[8,128]{1,0:T(8,128)(2,1)S(1)}, bf16[8,128]{1,0:T(8,128)(2,1)S(1)}, u32[]{:S(2)}, u32[]{:S(2)}) collective-permute-start(bf16[8,128]{1,0:T(8,128)(2,1)S(1)} %bitcast.88), channel_id=1, source_target_pairs={{0,8},{1,9},{2,10},{3,11},{4,12},{5,13},{6,14},{7,15},{8,0},{9,1},... | collective-permute-start | bytes 6152 | tf_op jit(solution)/shard_map/ppermute | solution.py:22
  183.5 80.6 %collective-permute-start.4 = (bf16[16,128]{1,0:T(8,128)(2,1)S(1)}, bf16[16,128]{1,0:T(8,128)(2,1)S(1)}, u32[]{:S(2)}, u32[]{:S(2)}) collective-permute-start(bf16[16,128]{1,0:T(8,128)(2,1)S(1)} %get-tuple-element.77), channel_id=1, source_target_pairs={{0,16},{1,17},{2,18},{3,19},{4,20},{5,21},{6,22},{7,23},{8,24},{9,... | collective-permute-start | bytes 12296 | tf_op jit(solution)/shard_map/ppermute | solution.py:22
  264.7 9.2 %all-to-all-start.1 = ((bf16[8,8,512]{2,0,1:T(8,128)(2,1)}), bf16[8,8,512]{2,0,1:T(8,128)(2,1)S(1)}, u32[]{:S(2)}, u32[]{:S(2)}) async-start(bf16[8,8,512]{2,0,1:T(8,128)(2,1)} %bitcast.11), calls=%async_computation.1 | async-start | bytes 131072 | tf_op jit(solution)/shard_map/all_to_all | solution.py:84
  300.0 8.7 %copy-start.1 = (f32[2,32,32,16]{1,3,2,0:T(8,128)S(1)}, f32[2,32,32,16]{1,3,2,0:T(8,128)}, u32[]{:S(2)}) copy-start(f32[2,32,32,16]{1,3,2,0:T(8,128)} %custom-call) | copy-start | bytes 393220
  308.8 31.4 %copy-start.2 = (bf16[1,8,4096]{2,1,0:T(8,128)(2,1)S(1)}, bf16[1,8,4096]{2,1,0:T(8,128)(2,1)}, u32[]{:S(2)}) copy-start(bf16[1,8,4096]{2,1,0:T(8,128)(2,1)} %param.11) | copy-start | bytes 196612
  330.0 10.1 %all-to-all-start.2 = ((f32[8,8,512]{2,1,0:T(8,128)}), f32[8,8,512]{2,1,0:T(8,128)S(1)}, u32[]{:S(2)}, u32[]{:S(2)}) async-start(f32[8,8,512]{2,1,0:T(8,128)} %all_to_all.50), calls=%async_computation.2 | async-start | bytes 262144 | tf_op jit(solution)/shard_map/all_to_all | solution.py:111
